TPU v7x, 256 devices: a whole 4x4x8 slice. The times are simulated.
256 devices in a mesh: prow: 32 (over z_hi, y, x), pcol: 8 (over z_lo, core).
Axes of the slice: x: 4, y: 4, z: 8 (z_hi: 2, z_lo: 4; z = z_hi * 4 + z_lo), core: 2. Of those that a mesh axis runs over, the one named last changes fastest.
Arguments:
- eigen_rows: float32 [1024, 229376], P(('pcol', 'prow')), may hold values from -6 to 6
- reflectors: float32 [229376, 512], P('prow', 'pcol'), may hold values from -0.375 to 0.375
- tfactors: float32 [2, 256, 256], replicated, may hold values from -0.01171875 to 0.01171875
Outputs:
- back_rows: float32 [1024, 229376], P('pcol', 'prow')
All inputs are finite; a program needn't handle non-finite values.
Results may differ from a plain program's by a relative error of at most 0.000084.
Values sent between devices are 32-bit elements; how exact they have to be, the bound alone decides.
No kernel may reach another device: no remote copies, remote signals or barrier semaphores. Data moves between devices by JAX's collectives and lax.ppermute only.
A program may use at most 128 MiB of HBM per device.

v0:
```python
import jax
import jax.numpy as jnp
from jax import lax
from jax.sharding import PartitionSpec as P


def upper_part(square):
    width = square.shape[0]
    rows = lax.broadcasted_iota(jnp.int32, (width, width), 0)
    cols = lax.broadcasted_iota(jnp.int32, (width, width), 1)
    return jnp.where(cols >= rows, square, jnp.zeros_like(square))


def matmul(left, right):
    return jnp.dot(left, right, precision=lax.Precision.HIGHEST, preferred_element_type=jnp.float32)


def apply_both(matrix, vectors, tfactors, summer):
    width = tfactors.shape[1]
    first_tri = upper_part(tfactors[0])
    second_tri = upper_part(tfactors[1])
    for panel_index in (1, 0):
        panel_vectors = vectors[:, panel_index * width : (panel_index + 1) * width]
        triangle = second_tri if panel_index == 1 else first_tri
        projected = summer(matmul(matrix, panel_vectors))
        matrix = matrix - matmul(matmul(projected, triangle.T), panel_vectors.T)
    return matrix


def body(eigen_rows, reflectors, tfactors):
    grid_rows = lax.all_to_all(eigen_rows, "prow", split_axis=1, concat_axis=0, tiled=True)
    grid_vectors = lax.all_gather(reflectors, "pcol", axis=1, tiled=True)

    def summer_grid(values):
        return lax.psum(values, "prow")

    return apply_both(grid_rows, grid_vectors, tfactors, summer_grid)


def solution(mesh):
    return jax.shard_map(
        body,
        mesh=mesh,
        in_specs=(P(("pcol", "prow"), None), P("prow", "pcol"), P()),
        out_specs=P("pcol", "prow"),
        check_vma=False,
    )
```

profile of v0, /device:TPU:32, one launch (start us, length us, event | category | flops | bytes accessed | tf_op | source)
XLA Modules:
  0.0 1083.6 jit_solution(4444081856075703498)
XLA Ops:
  6.5 0.0 all-gather.2.cloned.1.call-start
  6.5 0.7 all-gather.2.cloned.1.call-update
  7.3 0.0 all-reduce.3.cloned.1.call-start
  7.3 139.8 %all_to_all.19 = f32[4,32,7168]{2,0,1:T(4,128)} all-to-all(f32[4,32,7168]{2,0,1:T(4,128)} %bitcast.15), channel_id=1, replica_groups=mesh['prow'=32,'pcol'=8] {'prow'}, dimensions={1} | all-to-all | bytes 7340032 | tf_op jit(solution)/shard_map/all_to_all | solution.py:31
  147.1 5.3 all_to_all.17
  152.3 0.0 copy-start.2
  152.3 86.0 %all-gather.2.cloned.1.call-done = f32[7168,512]{0,1:T(8,128)} async-done(((f32[7168,64]{0,1:T(8,128)}), f32[7168,512]{0,1:T(8,128)}) %all-gather.2.cloned.1.call-update) | async-done | bytes 14680080 | tf_op jit(solution)/shard_map/all_gather | solution.py:32
  238.4 12.3 %fusion.4 = f32[128,256]{1,0:T(8,128)} fusion(f32[128,7168]{1,0:T(8,128)} %all_to_all.17, f32[7168,512]{0,1:T(8,128)} %all-gather.2.cloned.1.call-done), kind=kOutput, calls=%fused_computation.6 | convolution fusion | flops 2818572288 | bytes 11141120 | tf_op jit(solution)/shard_map/dot_general | solution.py:15
  250.6 0.0 all-reduce.3.cloned.1.call-update
  250.6 0.2 all-reduce.5.cloned.1.call-start
  250.9 398.6 %all-reduce.3.cloned.1.call-done = f32[128,256]{1,0:T(8,128)} async-done(((f32[128,256]{1,0:T(8,128)}), f32[128,256]{1,0:T(8,128)}) %all-reduce.3.cloned.1.call-update) | async-done | bytes 131088 | tf_op jit(solution)/shard_map/psum | solution.py:35
  649.4 0.0 copy-done.2
  649.4 1.3 fusion.7
  650.7 0.0 copy-start
  650.8 9.2 convolution_subtract_fusion.1
  660.0 0.0 copy-start.1
  660.0 1.8 copy-done.1
  661.8 0.0 copy-done
  661.8 8.1 fusion.1
  669.9 0.0 all-reduce.5.cloned.1.call-update
  669.9 395.6 %all-reduce.5.cloned.1.call-done = f32[128,256]{1,0:T(8,128)} async-done(((f32[128,256]{1,0:T(8,128)}), f32[128,256]{1,0:T(8,128)}) %all-reduce.5.cloned.1.call-update) | async-done | bytes 131088 | tf_op jit(solution)/shard_map/psum | solution.py:35
  1065.4 1.3 fusion.6
  1066.8 10.3 convolution_subtract_fusion
Async XLA Ops:
  6.5 231.8 %all-gather.2.cloned.1.call-start = ((), (), s32[]{:S(2)}) async-start(), calls=%async_computation.1 | async-start | bytes 16515072 | tf_op jit(solution)/shard_map/all_gather | solution.py:32
  7.3 642.2 %all-reduce.3.cloned.1.call-start = ((), (), s32[]{:S(2)}) async-start(), calls=%async_computation.2 | async-start | bytes 262144 | tf_op jit(solution)/shard_map/psum | solution.py:35
  152.3 497.1 %copy-start.2 = (f32[2,256,256]{2,1,0:T(8,128)S(1)}, f32[2,256,256]{2,1,0:T(8,128)}, u32[]{:S(2)}) copy-start(f32[2,256,256]{2,1,0:T(8,128)} %param.5) | copy-start | bytes 1572868
  250.6 814.8 %all-reduce.5.cloned.1.call-start = ((), (), s32[]{:S(2)}) async-start(), calls=%async_computation.3 | async-start | bytes 262144 | tf_op jit(solution)/shard_map/psum | solution.py:35
  650.7 11.1 %copy-start = (f32[7168,512]{0,1:T(8,128)S(1)}, f32[7168,512]{0,1:T(8,128)}, u32[]{:S(2)}) copy-start(f32[7168,512]{0,1:T(8,128)} %all-gather.2.cloned.1.call-done) | copy-start | bytes 44040196
  660.0 1.8 copy-start.1
Sparse Core Ops, SparseCore 0:
  9.1 229.1 all-gather.1
  250.8 398.6 all-reduce.2
  670.0 395.3 all-reduce.4
where the time goes:
time: 1080 us
  waiting for transfers between devices  881 us (82%)
  blocking collectives  140 us (13%)
  matrix products  42.4 us (4%)
  between operations  13.2 us (1%)
    psum x2, waiting for transfers between devices, summer_grid(): return lax.psum(values, 'prow')  794 us
    all_to_all x1, blocking collectives, body(): lax.all_to_all(eigen_rows, 'prow', split_axis=1, concat_axis=0, tiled=True)  140 us
    all_gather x1, waiting for transfers between devices, body(): grid_vectors = lax.all_gather(reflectors, 'pcol', axis=1, tiled=True)  86 us
    dot_general x6, matrix products, matmul(): jnp.dot(left, right, precision=lax.Precision.HIGHEST, preferred_element_t...  42.4 us
  transfers between devices with their start and end apart: 3, of which 3 were waited for; matrix products, arithmetic and copies ran while one was open for 0% of the time, Pallas kernels for 0%

commit v1 on v0

--- a/solution.py
+++ b/solution.py
@@ -32,7 +32,7 @@
     grid_vectors = lax.all_gather(reflectors, "pcol", axis=1, tiled=True)
 
     def summer_grid(values):
-        return lax.psum(values, "prow")
+        return jnp.sum(lax.all_gather(values, "prow"), axis=0)
 
     return apply_both(grid_rows, grid_vectors, tfactors, summer_grid)
 

time: 1080 us -> 511 us (0.47)
  waiting for transfers between devices: 881 us -> 305 us
    psum x2 -> x0, waiting for transfers between devices: 794 us -> none  [summer_grid(): return lax.psum(values, 'prow')]
    all_gather x0 -> x2, waiting for transfers between devices: none -> 219 us  [summer_grid(): return jnp.sum(lax.all_gather(values, 'prow'), axis=0)]
where the time goes in v1:
time: 511 us
  waiting for transfers between devices  305 us (60%)
  blocking collectives  140 us (27%)
  matrix products  40.6 us (8%)
  between operations  13.2 us (3%)
  local copies, waits for them, and re-layouts  7.1 us (1%)
    all_gather x2, waiting for transfers between devices, summer_grid(): return jnp.sum(lax.all_gather(values, 'prow'), axis=0)  219 us
    all_to_all x1, blocking collectives, body(): lax.all_to_all(eigen_rows, 'prow', split_axis=1, concat_axis=0, tiled=True)  140 us
    all_gather x1, waiting for transfers between devices, body(): grid_vectors = lax.all_gather(reflectors, 'pcol', axis=1, tiled=True)  86 us
    dot_general x6, matrix products, matmul(): jnp.dot(left, right, precision=lax.Precision.HIGHEST, preferred_element_t...  40.6 us
  transfers between devices with their start and end apart: 3, of which 3 were waited for; matrix products, arithmetic and copies ran while one was open for 0% of the time, Pallas kernels for 0%

profile of v1, /device:TPU:32, one launch (start us, length us, event | category | flops | bytes accessed | tf_op | source)
XLA Modules:
  0.0 511.1 jit_solution(12965912151227493887)
XLA Ops:
  6.5 0.0 all-gather.6.cloned.1.call-start
  6.5 0.7 all-gather.6.cloned.1.call-update
  7.3 0.0 all-gather.8.cloned.1.call-start
  7.3 139.8 %all_to_all.19 = f32[4,32,7168]{2,0,1:T(4,128)} all-to-all(f32[4,32,7168]{2,0,1:T(4,128)} %bitcast.19), channel_id=1, replica_groups=mesh['prow'=32,'pcol'=8] {'prow'}, dimensions={1} | all-to-all | bytes 7340032 | tf_op jit(solution)/shard_map/all_to_all | solution.py:31
  147.1 5.3 %all_to_all.17 = f32[128,7168]{1,0:T(8,128)} reshape(f32[32,4,7168]{2,1,0:T(4,128)} %bitcast.16) | data formatting | bytes 7340032 | tf_op jit(solution)/shard_map/all_to_all | solution.py:31
  152.3 86.0 %all-gather.6.cloned.1.call-done = f32[7168,512]{0,1:T(8,128)} async-done(((f32[7168,64]{0,1:T(8,128)}), f32[7168,512]{0,1:T(8,128)}) %all-gather.6.cloned.1.call-update) | async-done | bytes 14680080 | tf_op jit(solution)/shard_map/all_gather | solution.py:32
  238.4 12.2 %fusion.4 = f32[128,256]{1,0:T(8,128)} fusion(f32[128,7168]{1,0:T(8,128)} %all_to_all.17, f32[7168,512]{0,1:T(8,128)} %all-gather.6.cloned.1.call-done), kind=kOutput, calls=%fused_computation.6 | convolution fusion | flops 2818572288 | bytes 11141120 | tf_op jit(solution)/shard_map/dot_general | solution.py:15
  250.6 0.0 all-gather.8.cloned.1.call-update
  250.6 0.2 all-gather.10.cloned.1.call-start
  250.9 112.7 %all-gather.8.cloned.1.call-done = f32[4096,256]{1,0:T(8,128)} async-done(((f32[128,256]{1,0:T(8,128)}), f32[4096,256]{1,0:T(8,128)}) %all-gather.8.cloned.1.call-update) | async-done | bytes 4194320 | tf_op jit(solution)/shard_map/all_gather | solution.py:35
  363.6 2.4 reduce_sum.18
  366.0 0.0 copy-done.2
  366.0 0.4 fusion.7
  366.4 0.0 copy-start
  366.4 9.2 %convolution_subtract_fusion.1 = f32[128,7168]{1,0:T(8,128)S(1)} fusion(f32[128,7168]{1,0:T(8,128)} %all_to_all.17, f32[128,256]{1,0:T(8,128)S(1)} %fusion.7, f32[7168,512]{0,1:T(8,128)} %all-gather.6.cloned.1.call-done), kind=kOutput, calls=%fused_computation.1 | convolution fusion | flops 2819489792 | bytes 14811136 | tf_op jit(solution)/shard_map/dot_general | solution.py:15
  375.6 0.0 copy-start.1
  375.7 1.8 copy-done.1
  377.5 0.0 copy-done
  377.5 8.0 %fusion.1 = f32[128,256]{1,0:T(8,128)} fusion(f32[128,7168]{1,0:T(8,128)S(1)} %convolution_subtract_fusion.1, f32[7168,512]{0,1:T(8,128)S(1)} %copy-done), kind=kOutput, calls=%fused_computation.3 | convolution fusion | flops 2818572288 | bytes 11141120 | tf_op jit(solution)/shard_map/dot_general | solution.py:15
  385.5 0.0 all-gather.10.cloned.1.call-update
  385.6 105.9 %all-gather.10.cloned.1.call-done = f32[4096,256]{1,0:T(8,128)} async-done(((f32[128,256]{1,0:T(8,128)}), f32[4096,256]{1,0:T(8,128)}) %all-gather.10.cloned.1.call-update) | async-done | bytes 4194320 | tf_op jit(solution)/shard_map/all_gather | solution.py:35
  491.4 2.4 reduce_sum.19
  493.9 0.4 fusion.6
  494.3 10.3 %convolution_subtract_fusion = f32[128,7168]{1,0:T(8,128)} fusion(f32[128,7168]{1,0:T(8,128)} %copy-done.1, f32[128,256]{1,0:T(8,128)S(1)} %fusion.6, f32[7168,512]{0,1:T(8,128)} %all-gather.6.cloned.1.call-done), kind=kOutput, calls=%fused_computation | convolution fusion | flops 2819489792 | bytes 14811136 | tf_op jit(solution)/shard_map/dot_general | solution.py:15
  (1 shorter events, 0.0 us)
Async XLA Ops:
  6.5 231.8 %all-gather.6.cloned.1.call-start = ((), (), s32[]{:S(2)}) async-start(), calls=%async_computation.1 | async-start | bytes 16515072 | tf_op jit(solution)/shard_map/all_gather | solution.py:32
  7.3 356.3 %all-gather.8.cloned.1.call-start = ((), (), s32[]{:S(2)}) async-start(), calls=%async_computation.2 | async-start | bytes 4325376 | tf_op jit(solution)/shard_map/all_gather | solution.py:35
  250.6 115.4 %copy-start.2 = (f32[2,256,256]{2,1,0:T(8,128)S(1)}, f32[2,256,256]{2,1,0:T(8,128)}, u32[]{:S(2)}) copy-start(f32[2,256,256]{2,1,0:T(8,128)} %param.5) | copy-start | bytes 1572868
  250.6 240.8 %all-gather.10.cloned.1.call-start = ((), (), s32[]{:S(2)}) async-start(), calls=%async_computation.3 | async-start | bytes 4325376 | tf_op jit(solution)/shard_map/all_gather | solution.py:35
  366.4 11.1 %copy-start = (f32[7168,512]{0,1:T(8,128)S(1)}, f32[7168,512]{0,1:T(8,128)}, u32[]{:S(2)}) copy-start(f32[7168,512]{0,1:T(8,128)} %all-gather.6.cloned.1.call-done) | copy-start | bytes 44040196
  375.6 1.8 copy-start.1
Sparse Core Ops, SparseCore 0:
  9.1 229.1 all-gather.5
  250.8 112.7 all-gather.7
  385.7 105.6 all-gather.9
